TPU v7x, 128 devices: a whole 4x4x4 slice. The times are simulated.
128 devices in a mesh: sub: 16 (over y, z), grp: 8 (over x, core).
Axes of the slice: x: 4, y: 4, z: 4, core: 2. Of those that a mesh axis runs over, the one named last changes fastest.
Arguments:
- interior_res: bfloat16 [1024, 32, 256], P(('sub', 'grp')), may hold values from -6 to 6
- interface_res: bfloat16 [1024, 32, 512], P(('sub', 'grp')), may hold values from -6 to 6
- interior_inv: bfloat16 [1024, 256, 256], P(('sub', 'grp')), may hold values from -0.375 to 0.375
- coupling: bfloat16 [1024, 512, 256], P(('sub', 'grp')), may hold values from -0.375 to 0.375
- schur_inv: bfloat16 [1024, 512, 512], P(('sub', 'grp')), may hold values from -0.25 to 0.25
- coarse_inv: bfloat16 [512, 128, 128], P('grp'), may hold values from -0.5 to 0.5
- coarse_part: int32 [524288, 1], P(('sub', 'grp')), may hold values from 0 to 127; in each aligned block of 4096 rows (0 to 4095, 4096 to 8191, ...) at most 64 rows name the same one
- coarse_slot: int32 [524288], P(('sub', 'grp')), may hold values from 0 to 511
- live_count: int32 [1024], P(('sub', 'grp')), may hold values from 128 to 512
Outputs:
- interior_update: bfloat16 [1024, 32, 256], P(('sub', 'grp'))
- interface_update: bfloat16 [1024, 32, 512], P(('sub', 'grp'))
Inputs may be any that keep to these rules, and one draw needn't show every extreme that they name: `coarse_part`: in each device's aligned block of 4096 rows no section is named by more than 64 rows, a bound that some block reaches.
All inputs are finite; a program needn't handle non-finite values.
Results may differ from a plain program's by a relative error of at most 0.0076.
Values may be sent and summed in bfloat16 or wider, within the bound.
No kernel may reach another device: no remote copies, remote signals or barrier semaphores. Data moves between devices by JAX's collectives and lax.ppermute only.
A program may use at most 64 MiB of HBM per device.

v0:
```python
import math
import jax
import jax.numpy as jnp
from jax import lax
from jax.sharding import PartitionSpec as P


def coarse_apply(right_side, inverse_blocks):
    vec_count = right_side.shape[0]
    block_size = inverse_blocks.shape[1]
    reshaped = right_side.reshape(vec_count, -1, block_size)
    solved = jnp.einsum(
        "kbj,bij->kbi", reshaped, inverse_blocks, preferred_element_type=jnp.float32
    )
    return solved.reshape(vec_count, -1).astype(jnp.bfloat16)


def spread_cols(values, target, total):
    width = math.gcd(total, 512)

    def spread_one_block(number):
        columns = number * width + lax.iota(jnp.int32, width)
        table = (target[:, None] == columns[None, :]).astype(jnp.bfloat16)
        return jnp.dot(values, table, preferred_element_type=jnp.float32)

    blocks = lax.map(spread_one_block, jnp.arange(total // width, dtype=jnp.int32))
    return jnp.transpose(blocks, (1, 0, 2)).reshape(values.shape[0], total)


def pick_cols(values, wanted):
    count = wanted.shape[0]
    width = math.gcd(count, 512)
    source = lax.iota(jnp.int32, values.shape[1])

    def pick_one_block(number):
        chosen = lax.dynamic_slice_in_dim(wanted, number * width, width, 0)
        table = (source[:, None] == chosen[None, :]).astype(jnp.bfloat16)
        return jnp.dot(values, table, preferred_element_type=jnp.float32)

    blocks = lax.map(pick_one_block, jnp.arange(count // width, dtype=jnp.int32))
    return jnp.transpose(blocks, (1, 0, 2)).reshape(values.shape[0], count).astype(jnp.bfloat16)


def place_in_section(section_list, sections):
    rows_dev = section_list.shape[0]
    width = math.gcd(rows_dev, 128)
    section_hot = (section_list[:, None] == jnp.arange(sections, dtype=jnp.int32)[None, :]).astype(
        jnp.float32
    )
    hot_blocks = section_hot.reshape(rows_dev // width, width, sections)
    lower = (
        lax.broadcasted_iota(jnp.int32, (width, width), 0)
        >= lax.broadcasted_iota(jnp.int32, (width, width), 1)
    ).astype(jnp.float32)
    within = jnp.einsum("ij,bjs->bis", lower, hot_blocks, precision=lax.Precision.HIGHEST)
    totals = within[:, -1, :]
    before = jnp.cumsum(totals, axis=0) - totals
    counted = (within + before[:, None, :]).reshape(rows_dev, sections)
    return jnp.sum((counted - 1.0) * section_hot, axis=1).astype(jnp.int32)


def with_slots(flattened, slot_values):
    upper = (slot_values // 256).astype(jnp.bfloat16)[None, :]
    lower = (slot_values % 256).astype(jnp.bfloat16)[None, :]
    return jnp.concatenate([flattened, upper, lower], axis=0)


def read_slots(received, vec_count):
    upper = received[vec_count].astype(jnp.int32)
    lower = received[vec_count + 1].astype(jnp.int32)
    return (received[:vec_count], upper * 256 + lower)


def on_device(
    interior_res,
    interface_res,
    interior_inv,
    coupling,
    schur_inv,
    coarse_inv,
    coarse_part,
    coarse_slot,
    live_count,
):
    sub_count, vec_count, interior = interior_res.shape
    boundary = interface_res.shape[2]
    owners = lax.axis_size("grp")
    subgroups = lax.axis_size("sub")
    sections = owners * subgroups
    rows_dev = sub_count * boundary
    capacity = 2 * rows_dev // sections
    piece_size = rows_dev // 8
    per_owner = coarse_inv.shape[0] * coarse_inv.shape[1]
    interior_pre = jnp.einsum(
        "sij,skj->ski", interior_inv, interior_res, preferred_element_type=jnp.float32
    ).astype(jnp.bfloat16)
    condensed = interface_res.astype(jnp.float32) - jnp.einsum(
        "sbi,ski->skb", coupling, interior_pre, preferred_element_type=jnp.float32
    )
    alive_mask = (
        lax.broadcasted_iota(jnp.int32, (sub_count, 1, boundary), 2) < live_count[:, None, None]
    )
    condensed = jnp.where(alive_mask, condensed, 0.0).astype(jnp.bfloat16)
    section_list = coarse_part[:, 0]
    owner_list = section_list % owners
    piece_list = section_list // owners
    position = place_in_section(section_list, sections)
    flattened = jnp.transpose(condensed, (1, 0, 2)).reshape(vec_count, rows_dev)
    destination = owner_list * (subgroups * capacity) + piece_list * capacity + position
    owner_slot = piece_list * piece_size + coarse_slot
    outgoing = spread_cols(
        with_slots(flattened, owner_slot), destination, sections * capacity
    ).astype(jnp.bfloat16)
    received = lax.all_to_all(outgoing, "grp", split_axis=1, concat_axis=1, tiled=True)
    recv_rows, recv_slots = read_slots(received, vec_count)
    partial_sum = spread_cols(recv_rows, recv_slots, per_owner)
    summed = lax.psum(partial_sum, "sub")
    coarse_sol = coarse_apply(summed.astype(jnp.bfloat16), coarse_inv)
    replies = pick_cols(coarse_sol, recv_slots)
    returned = lax.all_to_all(replies, "grp", split_axis=1, concat_axis=1, tiled=True)
    correction = pick_cols(returned, destination)
    correction = jnp.transpose(correction.reshape(vec_count, sub_count, boundary), (1, 0, 2))
    local_term = jnp.einsum(
        "sbc,skc->skb", schur_inv, condensed, preferred_element_type=jnp.float32
    )
    interface_update = jnp.where(
        alive_mask, local_term + correction.astype(jnp.float32), 0.0
    ).astype(jnp.bfloat16)
    extended = interior_res.astype(jnp.float32) - jnp.einsum(
        "sbi,skb->ski", coupling, interface_update, preferred_element_type=jnp.float32
    )
    interior_update = jnp.einsum(
        "sij,skj->ski",
        interior_inv,
        extended.astype(jnp.bfloat16),
        preferred_element_type=jnp.float32,
    ).astype(jnp.bfloat16)
    return (interior_update, interface_update)


def solution(mesh):
    in_specs = (
        P(("sub", "grp"), None, None),
        P(("sub", "grp"), None, None),
        P(("sub", "grp"), None, None),
        P(("sub", "grp"), None, None),
        P(("sub", "grp"), None, None),
        P("grp", None, None),
        P(("sub", "grp"), None),
        P(("sub", "grp")),
        P(("sub", "grp")),
    )
    out_specs = (P(("sub", "grp"), None, None), P(("sub", "grp"), None, None))
    return jax.shard_map(
        on_device, mesh=mesh, in_specs=in_specs, out_specs=out_specs, check_vma=False
    )
```

profile of v0, /device:TPU:1, one launch (start us, length us, event | category | flops | bytes accessed | tf_op | source)
XLA Modules:
  0.0 473.6 jit_solution(12313746118868401771)
XLA Ops:
  10.9 69.0 %while.46 = (s32[]{:T(128)}, bf16[16,34,512]{2,1,0:T(8,128)(2,1)}, s32[4096]{0:T(1024)}, s32[16]{0:T(128)S(1)}, bf16[34,4096]{1,0:T(8,128)(2,1)}, /*index=5*/s32[1]{0:T(128)}) while((s32[]{:T(128)}, bf16[16,34,512]{2,1,0:T(8,128)(2,1)}, s32[4096]{0:T(1024)}, s32[16]{0:T(128)S(1)}, bf16[34,4096]{1,0:T(8,128)(2,1)}, ...), condition=%wide.region_3.4_spmd.clone, body=%wide.region_2.3_spmd.sunk.clone | while | flops 144704000 | bytes 430689 | solution.py:26
  86.2 5.8 %all-to-all-start = ((bf16[34,8,1024]{2,0,1:T(8,128)(2,1)}), bf16[34,8,1024]{2,0,1:T(8,128)(2,1)}, u32[]{:S(2)}, u32[]{:S(2)}) async-start(bf16[34,8,1024]{2,0,1:T(8,128)(2,1)} %copy.27), calls=%async_computation | async-start | bytes 1310720 | tf_op jit(solution)/shard_map/all_to_all | solution.py:114
  92.8 10.0 %all-to-all-done = bf16[34,8,1024]{2,0,1:T(8,128)(2,1)} async-done(((bf16[34,8,1024]{2,0,1:T(8,128)(2,1)}), bf16[34,8,1024]{2,0,1:T(8,128)(2,1)}, u32[]{:S(2)}, u32[]{:S(2)}) %all-to-all-start) | async-done | bytes 557088 | tf_op jit(solution)/shard_map/all_to_all | solution.py:114
  106.5 88.7 %while.47 = (s32[]{:T(128)}, f32[16,32,512]{2,1,0:T(8,128)}, s32[8192]{0:T(1024)}, s32[16]{0:T(128)S(1)}, bf16[32,8192]{1,0:T(8,128)(2,1)}, /*index=5*/s32[1]{0:T(128)}) while((s32[]{:T(128)}, f32[16,32,512]{2,1,0:T(8,128)}, s32[8192]{0:T(1024)}, s32[16]{0:T(128)S(1)}, bf16[32,8192]{1,0:T(8,128)(2,1)}, /*index=5*/s32[1]{0:T(128)}) %tuple.96), condition=%wide.region_5.6_spmd.clone, body=%wide.region_4.5_spmd.sunk.clone | while | flops 272630272 | bytes 627297 | solution.py:26
  107.7 4.4 fusion.97
  113.2 4.4 fusion.97
  118.8 4.4 fusion.97
  124.3 4.4 fusion.97
  129.9 4.4 fusion.97
  135.4 4.4 fusion.97
  140.9 4.4 fusion.97
  146.5 4.4 fusion.97
  152.0 4.4 fusion.97
  157.6 4.4 fusion.97
  168.7 4.4 fusion.97
  174.2 4.4 fusion.97
  179.8 4.4 fusion.97
  185.3 4.4 fusion.97
  190.9 4.4 fusion.97
  197.6 76.3 %all-reduce.1 = bf16[32,8192]{1,0:T(8,128)(2,1)} all-reduce(f32[32,8192]{1,0:T(8,128)} %bitcast.120), channel_id=1, replica_groups=mesh['sub'=16,'grp'=8] {'sub'}, use_global_device_ids=true, to_apply=%region_6.7 | all-reduce | flops 262144 | bytes 1572864 | tf_op jit(solution)/shard_map/psum | solution.py:117
  277.0 101.6 %while.48 = (s32[]{:T(128)}, bf16[16,32,512]{2,1,0:T(8,128)(2,1)}, s32[16]{0:T(128)S(1)}, s32[8192]{0:T(1024)}, bf16[32,8192]{1,0:T(8,128)(2,1)}, /*index=5*/s32[1]{0:T(128)}) while((s32[]{:T(128)}, bf16[16,32,512]{2,1,0:T(8,128)(2,1)}, s32[16]{0:T(128)S(1)}, s32[8192]{0:T(1024)}, bf16[32,8192]{1,0:T(8,128)(2,1)}, ...), condition=%wide.region_8.9_spmd.clone.clone, body=%wide.region_7.8_spmd.clone.sunk.clone | while | flops 272629760 | bytes 596611 | solution.py:40
  384.9 19.1 %all-to-all-start.1 = ((bf16[32,8,1024]{2,0,1:T(8,128)(2,1)}), bf16[32,8,1024]{2,0,1:T(8,128)(2,1)}, u32[]{:S(2)}, u32[]{:S(2)}) async-start(bf16[32,8,1024]{2,0,1:T(8,128)(2,1)} %copy.33), calls=%async_computation.1 | async-start | bytes 1048576 | tf_op jit(solution)/shard_map/all_to_all | solution.py:120
  404.0 9.5 %all-to-all-done.1 = bf16[32,8,1024]{2,0,1:T(8,128)(2,1)} async-done(((bf16[32,8,1024]{2,0,1:T(8,128)(2,1)}), bf16[32,8,1024]{2,0,1:T(8,128)(2,1)}, u32[]{:S(2)}, u32[]{:S(2)}) %all-to-all-start.1) | async-done | bytes 524320 | tf_op jit(solution)/shard_map/all_to_all | solution.py:120
  415.3 50.9 %while.49 = (s32[]{:T(128)}, bf16[8,32,512]{2,1,0:T(8,128)(2,1)}, s32[8]{0:T(128)S(1)}, s32[4096]{0:T(1024)}, bf16[32,8192]{1,0:T(8,128)(2,1)}, /*index=5*/s32[1]{0:T(128)}) while((s32[]{:T(128)}, bf16[8,32,512]{2,1,0:T(8,128)(2,1)}, s32[8]{0:T(128)S(1)}, s32[4096]{0:T(1024)}, bf16[32,8192]{1,0:T(8,128)(2,1)}, ...), condition=%wide.region_10.11_spmd.clone.clone, body=%wide.region_9.10_spmd.clone.sunk.clone | while | flops 272629760 | bytes 596611 | solution.py:40
  (201 shorter events, 251.1 us)
Async XLA Ops:
  0.6 273.3 %copy-start = (bf16[64,128,128]{2,1,0:T(8,128)(2,1)S(1)}, bf16[64,128,128]{2,1,0:T(8,128)(2,1)}, u32[]{:S(2)}) copy-start(bf16[64,128,128]{2,1,0:T(8,128)(2,1)} %param.22) | copy-start | bytes 6291460
  0.6 1.8 copy-start.3
  0.7 3.1 copy-start.5
  0.7 4.4 copy-start.6
  0.7 5.0 %copy-start.1 = (bf16[8,256,256]{2,1,0:T(8,128)(2,1)S(1)}, bf16[8,256,256]{2,1,0:T(8,128)(2,1)}, u32[]{:S(2)}) copy-start(bf16[8,256,256]{2,1,0:T(8,128)(2,1)} %param.19) | copy-start | bytes 3145732
  0.7 5.0 %copy-start.2 = (bf16[8,32,256]{2,1,0:T(8,128)(2,1)S(1)}, bf16[8,32,256]{2,1,0:T(8,128)(2,1)}, u32[]{:S(2)}) copy-start(bf16[8,32,256]{2,1,0:T(8,128)(2,1)} %param.17) | copy-start | bytes 393220
  86.2 16.6 %all-to-all-start = ((bf16[34,8,1024]{2,0,1:T(8,128)(2,1)}), bf16[34,8,1024]{2,0,1:T(8,128)(2,1)}, u32[]{:S(2)}, u32[]{:S(2)}) async-start(bf16[34,8,1024]{2,0,1:T(8,128)(2,1)} %copy.27), calls=%async_computation | async-start | bytes 1310720 | tf_op jit(solution)/shard_map/all_to_all | solution.py:114
  384.9 28.5 %all-to-all-start.1 = ((bf16[32,8,1024]{2,0,1:T(8,128)(2,1)}), bf16[32,8,1024]{2,0,1:T(8,128)(2,1)}, u32[]{:S(2)}, u32[]{:S(2)}) async-start(bf16[32,8,1024]{2,0,1:T(8,128)(2,1)} %copy.33), calls=%async_computation.1 | async-start | bytes 1048576 | tf_op jit(solution)/shard_map/all_to_all | solution.py:120
  415.3 50.9 %copy-start.4 = (pred[8,512]{1,0:T(8,128)(4,1)S(1)}, pred[8,512]{1,0:T(8,128)(4,1)}, u32[]{:S(2)}) copy-start(pred[8,512]{1,0:T(8,128)(4,1)} %iota_compare_fusion.17) | copy-start | bytes 12292
where the time goes:
time: 477 us; the launch traced here: 474 us
  matrix products  238 us (50%)
  blocking collectives  76.3 us (16%)
  local copies, waits for them, and re-layouts  71.9 us (15%)
  loops' own time  35.1 us (7%)
  starting transfers between devices  24.8 us (5%)
  waiting for transfers between devices  19.5 us (4%)
  other arithmetic  7.01 us (1%)
    dot_general x32, matrix products, spread_one_block(): return jnp.dot(values, table, preferred_element_type=jnp.float32)  119 us
    dot_general x24, matrix products, pick_one_block(): return jnp.dot(values, table, preferred_element_type=jnp.float32)  105 us
    psum x1, blocking collectives, on_device(): summed = lax.psum(partial_sum, 'sub')  76.3 us
    dynamic_slice x48, local copies, waits for them, and re-layouts, spread_cols(): lax.map(spread_one_block, jnp.arange(total // width, dtype=jnp.int32))  28 us
    another operation x2, loops' own time, spread_cols(): lax.map(spread_one_block, jnp.arange(total // width, dtype=jnp.int32))  19.7 us
    all_to_all x1, starting transfers between devices, on_device(): lax.all_to_all(replies, 'grp', split_axis=1, concat_axis=1, tiled=True)  19.1 us
    dynamic_slice x24, local copies, waits for them, and re-layouts, pick_one_block(): chosen = lax.dynamic_slice_in_dim(wanted, number * width, width, 0)  18.2 us
    another operation x2, loops' own time, pick_cols(): lax.map(pick_one_block, jnp.arange(count // width, dtype=jnp.int32))  15.4 us
  transfers between devices with their start and end apart: 2, of which 2 were waited for; matrix products, arithmetic and copies ran while one was open for 0% of the time, Pallas kernels for 0%

commit v1 on v0

--- a/solution.py
+++ b/solution.py
@@ -114,7 +114,7 @@
     received = lax.all_to_all(outgoing, "grp", split_axis=1, concat_axis=1, tiled=True)
     recv_rows, recv_slots = read_slots(received, vec_count)
     partial_sum = spread_cols(recv_rows, recv_slots, per_owner)
-    summed = lax.psum(partial_sum, "sub")
+    summed = jnp.sum(lax.all_gather(partial_sum, "sub"), axis=0)
     coarse_sol = coarse_apply(summed.astype(jnp.bfloat16), coarse_inv)
     replies = pick_cols(coarse_sol, recv_slots)
     returned = lax.all_to_all(replies, "grp", split_axis=1, concat_axis=1, tiled=True)

time: 477 us -> 524 us (1.099)
  waiting for transfers between devices: 19.5 us -> 132 us
  blocking collectives: 76.3 us -> 0 us
  starting transfers between devices: 24.8 us -> 10.9 us
  between operations: 0.76 us -> 14.1 us
  other arithmetic: 7.01 us -> 14.6 us
    all_gather x0 -> x1, waiting for transfers between devices: none -> 111 us  [on_device(): summed = jnp.sum(lax.all_gather(partial_sum, 'sub'), axis=0)]
    psum x1 -> x0, blocking collectives: 76.3 us -> none  [on_device(): summed = lax.psum(partial_sum, 'sub')]
    all_to_all x1, starting transfers between devices: 19.1 us -> 5.09 us  [on_device(): lax.all_to_all(replies, 'grp', split_axis=1, concat_axis=1, tiled=True)]
    reduce_sum x0 -> x1, other arithmetic: none -> 7.51 us  [on_device(): summed = jnp.sum(lax.all_gather(partial_sum, 'sub'), axis=0)]
  transfers between devices with their start and end apart: 2 -> 3, of which waited for: 2 -> 3; matrix products, arithmetic and copies ran while one was open for 0% -> 0% of each run, Pallas kernels for 0% -> 0%
where the time goes in v1:
time: 524 us; the launch traced here: 520 us
  matrix products  238 us (45%)
  waiting for transfers between devices  132 us (25%)
  local copies, waits for them, and re-layouts  75.3 us (14%)
  loops' own time  35.6 us (7%)
  other arithmetic  14.6 us (3%)
  between operations  14.1 us (3%)
  starting transfers between devices  10.9 us (2%)
    dot_general x32, matrix products, spread_one_block(): return jnp.dot(values, table, preferred_element_type=jnp.float32)  119 us
    all_gather x1, waiting for transfers between devices, on_device(): summed = jnp.sum(lax.all_gather(partial_sum, 'sub'), axis=0)  111 us
    dot_general x24, matrix products, pick_one_block(): return jnp.dot(values, table, preferred_element_type=jnp.float32)  105 us
    dynamic_slice x48, local copies, waits for them, and re-layouts, spread_cols(): lax.map(spread_one_block, jnp.arange(total // width, dtype=jnp.int32))  28.5 us
    another operation x2, loops' own time, spread_cols(): lax.map(spread_one_block, jnp.arange(total // width, dtype=jnp.int32))  20.9 us
    dynamic_slice x24, local copies, waits for them, and re-layouts, pick_one_block(): chosen = lax.dynamic_slice_in_dim(wanted, number * width, width, 0)  18.3 us
    another operation x2, loops' own time, pick_cols(): lax.map(pick_one_block, jnp.arange(count // width, dtype=jnp.int32))  14.7 us
    all_to_all x1, waiting for transfers between devices, on_device(): lax.all_to_all(outgoing, 'grp', split_axis=1, concat_axis=1, tiled=True)  10.9 us
  transfers between devices with their start and end apart: 3, of which 3 were waited for; matrix products, arithmetic and copies ran while one was open for 0% of the time, Pallas kernels for 0%

profile of v1, /device:TPU:1, one launch (start us, length us, event | category | flops | bytes accessed | tf_op | source)
XLA Modules:
  0.0 520.5 jit_solution(7571896004683294192)
XLA Ops:
  17.4 69.0 %while.46 = (s32[]{:T(128)}, bf16[16,34,512]{2,1,0:T(8,128)(2,1)}, s32[4096]{0:T(1024)}, s32[16]{0:T(128)S(1)}, bf16[34,4096]{1,0:T(8,128)(2,1)}, /*index=5*/s32[1]{0:T(128)}) while((s32[]{:T(128)}, bf16[16,34,512]{2,1,0:T(8,128)(2,1)}, s32[4096]{0:T(1024)}, s32[16]{0:T(128)S(1)}, bf16[34,4096]{1,0:T(8,128)(2,1)}, ...), condition=%wide.region_3.4_spmd.clone, body=%wide.region_2.3_spmd.sunk.clone | while | flops 144704000 | bytes 430689 | solution.py:26
  92.7 5.8 %all-to-all-start = ((bf16[34,8,1024]{2,0,1:T(8,128)(2,1)}), bf16[34,8,1024]{2,0,1:T(8,128)(2,1)}, u32[]{:S(2)}, u32[]{:S(2)}) async-start(bf16[34,8,1024]{2,0,1:T(8,128)(2,1)} %copy.27), calls=%async_computation | async-start | bytes 1310720 | tf_op jit(solution)/shard_map/all_to_all | solution.py:114
  98.5 10.9 %all-to-all-done = bf16[34,8,1024]{2,0,1:T(8,128)(2,1)} async-done(((bf16[34,8,1024]{2,0,1:T(8,128)(2,1)}), bf16[34,8,1024]{2,0,1:T(8,128)(2,1)}, u32[]{:S(2)}, u32[]{:S(2)}) %all-to-all-start) | async-done | bytes 557088 | tf_op jit(solution)/shard_map/all_to_all | solution.py:114
  113.0 90.5 %while.47 = (s32[]{:T(128)}, f32[16,32,512]{2,1,0:T(8,128)}, s32[8192]{0:T(1024)}, s32[16]{0:T(128)S(1)}, bf16[32,8192]{1,0:T(8,128)(2,1)}, /*index=5*/s32[1]{0:T(128)}) while((s32[]{:T(128)}, f32[16,32,512]{2,1,0:T(8,128)}, s32[8192]{0:T(1024)}, s32[16]{0:T(128)S(1)}, bf16[32,8192]{1,0:T(8,128)(2,1)}, /*index=5*/s32[1]{0:T(128)}) %tuple.98), condition=%wide.region_5.6_spmd.clone, body=%wide.region_4.5_spmd.sunk.clone | while | flops 272630272 | bytes 627297 | solution.py:26
  114.3 4.4 fusion.97
  125.6 4.4 fusion.97
  131.3 4.4 fusion.97
  136.9 4.4 fusion.97
  142.6 4.4 fusion.97
  148.3 4.4 fusion.97
  153.9 4.4 fusion.97
  159.6 4.4 fusion.97
  170.9 4.4 fusion.97
  176.6 4.4 fusion.97
  182.2 4.4 fusion.97
  187.9 4.4 fusion.97
  193.5 4.4 fusion.97
  199.2 4.4 fusion.97
  209.8 111.3 %all-gather.2.cloned.1.call-done = f32[16,32,8192]{2,1,0:T(8,128)} async-done(((f32[1,32,8192]{2,1,0:T(8,128)}), f32[16,32,8192]{2,1,0:T(8,128)}) %all-gather.2.cloned.1.call-update) | async-done | bytes 16777232 | tf_op jit(solution)/shard_map/all_gather | solution.py:117
  321.0 7.5 %reduce_sum.19 = bf16[32,8192]{1,0:T(8,128)(2,1)} reduce(f32[16,32,8192]{2,1,0:T(8,128)} %all-gather.2.cloned.1.call-done, f32[]{:T(128)} %constant.99.clone.1), dimensions={0}, to_apply=%region_6.7 | reduce | flops 3932160 | bytes 17301508 | tf_op jit(solution)/shard_map/reduce_sum | solution.py:117
  331.7 101.0 %while.48 = (s32[]{:T(128)}, bf16[16,32,512]{2,1,0:T(8,128)(2,1)}, s32[16]{0:T(128)S(1)}, s32[8192]{0:T(1024)}, bf16[32,8192]{1,0:T(8,128)(2,1)}, /*index=5*/s32[1]{0:T(128)}) while((s32[]{:T(128)}, bf16[16,32,512]{2,1,0:T(8,128)(2,1)}, s32[16]{0:T(128)S(1)}, s32[8192]{0:T(1024)}, bf16[32,8192]{1,0:T(8,128)(2,1)}, ...), condition=%wide.region_8.9_spmd.clone.clone, body=%wide.region_7.8_spmd.clone.sunk.clone | while | flops 272629760 | bytes 596611 | solution.py:40
  438.9 5.1 all-to-all-start.1
  444.0 9.5 %all-to-all-done.1 = bf16[32,8,1024]{2,0,1:T(8,128)(2,1)} async-done(((bf16[32,8,1024]{2,0,1:T(8,128)(2,1)}), bf16[32,8,1024]{2,0,1:T(8,128)(2,1)}, u32[]{:S(2)}, u32[]{:S(2)}) %all-to-all-start.1) | async-done | bytes 524320 | tf_op jit(solution)/shard_map/all_to_all | solution.py:120
  455.3 50.9 %while.49 = (s32[]{:T(128)}, bf16[8,32,512]{2,1,0:T(8,128)(2,1)}, s32[8]{0:T(128)S(1)}, s32[4096]{0:T(1024)}, bf16[32,8192]{1,0:T(8,128)(2,1)}, /*index=5*/s32[1]{0:T(128)}) while((s32[]{:T(128)}, bf16[8,32,512]{2,1,0:T(8,128)(2,1)}, s32[8]{0:T(128)S(1)}, s32[4096]{0:T(1024)}, bf16[32,8192]{1,0:T(8,128)(2,1)}, ...), condition=%wide.region_10.11_spmd.clone.clone, body=%wide.region_9.10_spmd.clone.sunk.clone | while | flops 272629760 | bytes 596611 | solution.py:40
  (205 shorter events, 259.1 us)
Async XLA Ops:
  7.2 321.4 %copy-start = (bf16[64,128,128]{2,1,0:T(8,128)(2,1)S(1)}, bf16[64,128,128]{2,1,0:T(8,128)(2,1)}, u32[]{:S(2)}) copy-start(bf16[64,128,128]{2,1,0:T(8,128)(2,1)} %param.22) | copy-start | bytes 6291460
  7.2 1.8 copy-start.3
  7.2 3.1 copy-start.5
  7.2 4.4 copy-start.6
  7.2 5.0 copy-start.1
  7.2 5.0 copy-start.2
  92.7 16.6 %all-to-all-start = ((bf16[34,8,1024]{2,0,1:T(8,128)(2,1)}), bf16[34,8,1024]{2,0,1:T(8,128)(2,1)}, u32[]{:S(2)}, u32[]{:S(2)}) async-start(bf16[34,8,1024]{2,0,1:T(8,128)(2,1)} %copy.27), calls=%async_computation | async-start | bytes 1310720 | tf_op jit(solution)/shard_map/all_to_all | solution.py:114
  98.5 222.5 %all-gather.2.cloned.1.call-start = ((), (), s32[]{:S(2)}) async-start(), calls=%async_computation.2 | async-start | bytes 17825792 | tf_op jit(solution)/shard_map/all_gather | solution.py:117
  438.9 14.5 %all-to-all-start.1 = ((bf16[32,8,1024]{2,0,1:T(8,128)(2,1)}), bf16[32,8,1024]{2,0,1:T(8,128)(2,1)}, u32[]{:S(2)}, u32[]{:S(2)}) async-start(bf16[32,8,1024]{2,0,1:T(8,128)(2,1)} %copy.33), calls=%async_computation.1 | async-start | bytes 1048576 | tf_op jit(solution)/shard_map/all_to_all | solution.py:120
  455.3 51.0 %copy-start.4 = (pred[8,512]{1,0:T(8,128)(4,1)S(1)}, pred[8,512]{1,0:T(8,128)(4,1)}, u32[]{:S(2)}) copy-start(pred[8,512]{1,0:T(8,128)(4,1)} %iota_compare_fusion.17) | copy-start | bytes 12292
Sparse Core Ops, SparseCore 0:
  209.0 111.9 all-gather.1
